TPU v7x, 256 devices: a whole 4x4x8 slice. The times are simulated.
256 devices in a mesh: gx: 4 (over y), gy: 16 (over z, core), sa: 4 (over x).
Axes of the slice: x: 4, y: 4, z: 8, core: 2. Of those that a mesh axis runs over, the one named last changes fastest.
Arguments:
- tokens: bfloat16 [192, 4, 8192], P(None, None, 'gx'), may hold values from -6 to 6
- norm_gain: bfloat16 [8192], P('gx'), may hold values from 0.099609375 to 1.8984375
- w_query: bfloat16 [8192, 8192], P('gx', 'gy'), may hold values from -0.125 to 0.125
- w_keyval: bfloat16 [8192, 2048], P('gx', 'gy'), may hold values from -0.0625 to 0.0625
- w_out: bfloat16 [8192, 8192], P('gy', 'gx'), may hold values from -0.09375 to 0.09375
- paged_key_cache: bfloat16 [2048, 128, 1024], P(('gx', 'gy', 'sa')), may hold values from -256 to 256
- paged_value_cache: bfloat16 [2048, 128, 1024], P(('gx', 'gy', 'sa')), may hold values from -12 to 12
- lengths: int32 [192], replicated, may hold values from 1 to 8192, as said below
- slot_owner: int32 [2048], P(('gx', 'gy', 'sa')), may hold values from 0 to 191, as said below
- slot_page_number: int32 [2048], P(('gx', 'gy', 'sa')), may hold values from -1 to 63, as said below
Outputs:
- mixed: float32 [192, 4, 8192], P(None, None, ('gx', 'gy'))
- appended_key_value: bfloat16 [192, 4, 2048], P('gx', None, 'gy')
Inputs may be any that keep to these rules, and one draw needn't show every extreme that they name: `lengths`: in each group of 48 consecutive requests, 4 hold 4096 to 8192 positions, one of them exactly 8192, and the others 1 to 512, one of them exactly 512. Slot s belongs to group s // 512, and its owner is a request of that group (slot_owner[s] // 48 == s // 512). Every page p < ceil(lengths[r] / 128) of request r is held by exactly one slot; a slot that holds no page has slot_page_number -1 and the group's first request as owner. `slot_page_number`: laid out with slot_owner as stated there.
All inputs are finite; a program needn't handle non-finite values.
Results may differ from a plain program's by a relative error of at most 0.005.
The roundings to bfloat16 on the way count: a program that leaves them out, or rounds other values in their place, can miss the bound.
Values may be sent and summed in bfloat16 or wider, within the bound.
A program may use at most 128 MiB of HBM per device.

v0:
```python
import jax
import jax.numpy as jnp
from jax import lax
from jax.sharding import PartitionSpec as P

D = 8192
QUERY_HEADS = 64
KEY_VALUE_HEADS = 8
HEAD_ENTRIES = 128


rope_base = 500000.0
norm_eps = 1e-05
neg_fill = -1e30
precise = lax.Precision.HIGHEST


def apply_rotary(head_rows, token_positions):
    half_dim = head_rows.shape[-1] // 2
    exponent = jnp.arange(half_dim, dtype=jnp.float32) * (-2.0 / head_rows.shape[-1])
    inverse_freq = jnp.power(jnp.float32(rope_base), exponent)
    angles = token_positions.astype(jnp.float32)[..., None, None] * inverse_freq
    cosine = jnp.cos(angles)
    sine_value = jnp.sin(angles)
    front_half = head_rows[..., :half_dim]
    back_half = head_rows[..., half_dim:]
    return jnp.concatenate(
        [
            front_half * cosine - back_half * sine_value,
            back_half * cosine + front_half * sine_value,
        ],
        axis=-1,
    )


def local(
    tokens,
    norm_gain,
    w_query,
    w_keyval,
    w_out,
    paged_key_cache,
    paged_value_cache,
    lengths,
    slot_owner,
    slot_page_number,
):
    row_count = tokens.shape[0]
    step_count = tokens.shape[1]
    grouped_query_rows = row_count // lax.axis_size("gx")
    group_index = lax.axis_index("gx")
    column_count = lax.axis_size("gy")
    column_index = lax.axis_index("gy")
    heads_per_group = QUERY_HEADS // KEY_VALUE_HEADS
    own_heads = QUERY_HEADS // column_count
    key_row_width = KEY_VALUE_HEADS * HEAD_ENTRIES
    kv_columns = w_keyval.shape[1]
    query_columns = w_query.shape[1]
    slot_ordinal = paged_key_cache.shape[0]
    page_position_count = paged_key_cache.shape[1]
    score_scale = HEAD_ENTRIES ** (-0.5)
    gain_vector = norm_gain.astype(jnp.float32)
    group_lengths = lax.dynamic_slice_in_dim(
        lengths, group_index * grouped_query_rows, grouped_query_rows
    )
    local_request_owner = slot_owner - group_index * grouped_query_rows
    member_mask = (
        local_request_owner[None, :] == jnp.arange(grouped_query_rows, dtype=jnp.int32)[:, None]
    )
    member = member_mask.astype(jnp.float32)
    slot_length = jnp.take(group_lengths, local_request_owner)
    cache_positions = (
        slot_page_number[:, None] * page_position_count
        + jnp.arange(page_position_count, dtype=jnp.int32)[None, :]
    )
    live_slots = (slot_page_number[:, None] >= 0) & (cache_positions < slot_length[:, None])
    live_mask = live_slots[:, None, None, None, :]
    key_page_blocks = paged_key_cache.reshape(
        slot_ordinal, page_position_count, KEY_VALUE_HEADS, HEAD_ENTRIES
    )
    value_page_blocks = paged_value_cache.reshape(
        slot_ordinal, page_position_count, KEY_VALUE_HEADS, HEAD_ENTRIES
    )
    head_ids = column_index * own_heads + jnp.arange(own_heads, dtype=jnp.int32)
    kv_of_head = head_ids // heads_per_group
    as_float = tokens.astype(jnp.float32)
    squares = jnp.sum(as_float * as_float, axis=-1)
    square_total = lax.psum(squares, "gx")
    inverse_norm = lax.rsqrt(square_total / D + norm_eps)
    normed = (as_float * inverse_norm[..., None] * gain_vector).astype(jnp.bfloat16)
    query_term = jnp.einsum("ruk,kc->ruc", normed, w_query, preferred_element_type=jnp.float32)
    keyval_term = jnp.einsum("ruk,kc->ruc", normed, w_keyval, preferred_element_type=jnp.float32)
    projected = lax.psum_scatter(
        jnp.concatenate([query_term, keyval_term], axis=-1), "gx", scatter_dimension=0, tiled=True
    ).astype(jnp.bfloat16)
    query_all, key_value_total = (
        lax.all_gather(projected[..., :query_columns], "gy", axis=2, tiled=True),
        lax.all_gather(projected[..., query_columns:], "gy", axis=2, tiled=True),
    )
    step_ids = jnp.arange(step_count, dtype=jnp.int32)
    token_positions = group_lengths[:, None] + step_ids[None, :]
    rotated_query = apply_rotary(
        query_all.astype(jnp.float32).reshape(
            grouped_query_rows, step_count, QUERY_HEADS, HEAD_ENTRIES
        ),
        token_positions,
    ).astype(jnp.bfloat16)
    rotated_key = apply_rotary(
        key_value_total[..., :key_row_width]
        .astype(jnp.float32)
        .reshape(grouped_query_rows, step_count, KEY_VALUE_HEADS, HEAD_ENTRIES),
        token_positions,
    ).astype(jnp.bfloat16)
    fresh_value = key_value_total[..., key_row_width:].reshape(
        grouped_query_rows, step_count, KEY_VALUE_HEADS, HEAD_ENTRIES
    )
    appended = jnp.concatenate(
        [
            rotated_key.reshape(grouped_query_rows, step_count, key_row_width),
            key_value_total[..., key_row_width:],
        ],
        axis=-1,
    )
    appended_part = lax.dynamic_slice_in_dim(appended, column_index * kv_columns, kv_columns, 2)
    slot_queries = jnp.take(rotated_query, local_request_owner, axis=0).reshape(
        slot_ordinal, step_count, KEY_VALUE_HEADS, heads_per_group, HEAD_ENTRIES
    )
    scores = (
        jnp.einsum(
            "suhgd,sphd->suhgp", slot_queries, key_page_blocks, preferred_element_type=jnp.float32
        )
        * score_scale
    )
    scores = jnp.where(live_mask, scores, neg_fill)
    slot_top = jnp.max(scores, axis=-1)
    request_top = jnp.max(
        jnp.where(member_mask[:, :, None, None, None], slot_top[None], neg_fill), axis=1
    )
    slot_tops = jnp.take(request_top, local_request_owner, axis=0)
    weights = jnp.where(live_mask, jnp.exp(scores - slot_tops[..., None]), 0.0)
    slot_weight = jnp.sum(weights, axis=-1)
    slot_value = jnp.einsum(
        "suhgp,sphd->suhgd",
        weights.astype(jnp.bfloat16),
        value_page_blocks,
        preferred_element_type=jnp.float32,
    )
    request_total = jnp.einsum("rs,suhg->ruhg", member, slot_weight, precision=precise).reshape(
        grouped_query_rows, step_count, QUERY_HEADS
    )
    request_value = jnp.einsum("rs,suhgd->ruhgd", member, slot_value, precision=precise).reshape(
        grouped_query_rows, step_count, QUERY_HEADS, HEAD_ENTRIES
    )
    request_top = request_top.reshape(grouped_query_rows, step_count, QUERY_HEADS)
    top_all = lax.pmax(request_top, ("gy", "sa"))
    rescale = jnp.exp(request_top - top_all)
    scaled_total = request_total * rescale
    scaled_value = request_value * rescale[..., None]
    total_all, value_all = lax.psum((scaled_total, scaled_value), ("gy", "sa"))
    head_total = lax.dynamic_slice_in_dim(total_all, column_index * own_heads, own_heads, 2)
    head_value = lax.dynamic_slice_in_dim(value_all, column_index * own_heads, own_heads, 2)
    head_top = lax.dynamic_slice_in_dim(top_all, column_index * own_heads, own_heads, 2)
    query_own = lax.dynamic_slice_in_dim(rotated_query, column_index * own_heads, own_heads, 2)
    key_own = jnp.take(rotated_key, kv_of_head, axis=2)
    value_own = jnp.take(fresh_value, kv_of_head, axis=2)
    fresh_scores = (
        jnp.einsum("ruhd,rvhd->ruhv", query_own, key_own, preferred_element_type=jnp.float32)
        * score_scale
    )
    seen = step_ids[:, None] >= step_ids[None, :]
    seen_mask = seen[None, :, None, :]
    fresh_scores = jnp.where(seen_mask, fresh_scores, neg_fill)
    top_final = jnp.maximum(head_top, jnp.max(fresh_scores, axis=-1))
    fresh_weights = jnp.where(seen_mask, jnp.exp(fresh_scores - top_final[..., None]), 0.0)
    carry_factor = jnp.exp(head_top - top_final)
    denominator = head_total * carry_factor + jnp.sum(fresh_weights, axis=-1)
    numerator = head_value * carry_factor[..., None] + jnp.einsum(
        "ruhv,rvhd->ruhd",
        fresh_weights.astype(jnp.bfloat16),
        value_own,
        preferred_element_type=jnp.float32,
    )
    attended = (
        (numerator / denominator[..., None])
        .astype(jnp.bfloat16)
        .reshape(grouped_query_rows, step_count, own_heads * HEAD_ENTRIES)
    )
    projected_out = jnp.einsum(
        "ruk,kc->ruc",
        lax.all_gather(attended, "gx", axis=0, tiled=True),
        w_out,
        preferred_element_type=jnp.float32,
    )
    mixed_part = lax.psum_scatter(projected_out, "gy", scatter_dimension=2, tiled=True)
    return (mixed_part, appended_part)


def solution(mesh):
    in_specs = (
        P(None, None, "gx"),
        P("gx"),
        P("gx", "gy"),
        P("gx", "gy"),
        P("gy", "gx"),
        P(("gx", "gy", "sa"), None, None),
        P(("gx", "gy", "sa"), None, None),
        P(),
        P(("gx", "gy", "sa")),
        P(("gx", "gy", "sa")),
    )
    out_specs = (P(None, None, ("gx", "gy")), P("gx", None, "gy"))
    return jax.shard_map(local, mesh=mesh, in_specs=in_specs, out_specs=out_specs, check_vma=False)
```

profile of v0, /device:TPU:1, one launch (start us, length us, event | category | flops | bytes accessed | tf_op | source)
XLA Modules:
  0.0 810.3 jit_solution(6846426197113053983)
XLA Ops:
  7.2 3.7 fusion
  11.0 9.5 %psum.21 = f32[192,4]{0,1:T(4,128)S(1)} all-reduce(f32[192,4]{0,1:T(4,128)S(1)} %copy.183), channel_id=1, replica_groups=mesh['gx'=4,'gy'=16,'sa'=4] {'gx'}, use_global_device_ids=true, to_apply=%region_1.2 | all-reduce | flops 768 | bytes 6144 | tf_op jit(solution)/shard_map/psum | solution.py:88
  20.7 3.8 fusion.2
  24.6 3.5 fusion.5
  28.1 3.4 fusion.3
  31.5 1.5 pad_maximum_fusion.1
  33.1 33.9 %reduce-scatter.3.cloned.1.call-done = f32[48,4,640]{2,0,1:T(8,128)} async-done(((f32[192,4,640]{2,0,1:T(8,128)}), f32[48,4,640]{2,0,1:T(8,128)}) %reduce-scatter.3.cloned.1.call-update) | async-done | bytes 491536 | tf_op jit(solution)/shard_map/reduce_scatter | solution.py:93
  67.0 1.1 convert_element_type.43
  68.0 0.7 slice.43
  68.8 0.3 all-reduce.2.cloned.1.call-start
  69.1 3.6 copy.234
  72.7 3.6 copy.235
  76.4 0.6 gather_fusion
  77.3 0.8 multiply_cosine_fusion
  78.1 3.2 bitcast_bitcast_fusion.1
  81.3 1.5 bitcast_bitcast_fusion
  82.8 27.4 %all-gather.2.cloned.1.call-done = bf16[48,4,8192]{2,0,1:T(8,128)(2,1)} async-done(((bf16[48,4,512]{2,0,1:T(8,128)(2,1)}), bf16[48,4,8192]{2,0,1:T(8,128)(2,1)}) %all-gather.2.cloned.1.call-update) | async-done | bytes 3145744 | tf_op jit(solution)/shard_map/all_gather | solution.py:97
  110.2 2.6 reshape.184
  112.8 3.8 copy.233
  116.7 10.9 %fusion.58 = (f32[48,4,64,64]{3,2,0,1:T(8,128)}, f32[48,4,64,64]{3,2,0,1:T(8,128)}) fusion(f32[48,4,64,128]{3,2,0,1:T(8,128)} %bitcast.95), kind=kLoop, calls=%fused_computation.109 | loop fusion | bytes 12582912 | tf_op jit(solution)/shard_map/slice | solution.py:25
  127.6 15.6 %add_convert_fusion = (bf16[48,4,64,64]{3,1,2,0:T(4,128)(2,1)S(1)}, bf16[48,4,64,64]{3,1,2,0:T(4,128)(2,1)S(1)}) fusion(f32[48,4,64,64]{3,2,0,1:T(8,128)} %get-tuple-element.26, f32[48,4,64,64]{3,2,0,1:T(8,128)} %get-tuple-element.25, f32[48,4,64]{2,1,0:T(4,128)S(1)} %get-tuple-element.37, f32[48,4,64]{2,1,0:T(4,128)S(1)} %get-tuple-element.36), kind=kLoop, calls=%fused_computation.11 | loop fusion | flops 6291456 | bytes 9535488 | tf_op jit(solution)/shard_map/convert.3
  143.2 1.7 copy-done.1
  144.9 0.9 copy-done.2
  145.8 5.3 pad_maximum_fusion
  151.1 2.9 gather_fusion.1
  154.0 3.9 fusion.61
  157.9 0.3 select_reduce_fusion
  158.2 0.7 copy.192
  158.9 0.6 gather_fusion.2
  159.6 253.7 %pmax.7 = f32[48,4,64]{0,2,1:T(8,128)S(1)} all-reduce(f32[48,4,64]{0,2,1:T(8,128)S(1)} %bitcast.102), channel_id=1, replica_groups=mesh['gx'=4,'gy'=16,'sa'=4] {'gy','sa'}, use_global_device_ids=true, to_apply=%region_5.6 | all-reduce | flops 12288 | bytes 98304 | tf_op jit(solution)/shard_map/pmax | solution.py:155
  413.4 2.4 copy.196
  415.8 2.6 fusion.14
  418.5 2.8 fusion.29
  421.3 6.6 copy_multiply_fusion
  427.9 0.5 iota_compare_fusion.3
  428.4 0.3 copy-done.6
  428.7 0.6 copy.199
  429.4 0.6 copy.201
  430.0 21.8 %all_gather.10 = bf16[48,4,2048]{2,0,1:T(8,128)(2,1)S(1)} all-gather(bf16[48,4,128]{2,0,1:T(8,128)(2,1)S(1)} %slice.46), channel_id=1, replica_groups=mesh['gx'=4,'gy'=16,'sa'=4] {'gy'}, dimensions={2}, use_global_device_ids=true | all-gather | bytes 835584 | tf_op jit(solution)/shard_map/all_gather | solution.py:98
  452.1 0.8 copy.276
  452.9 0.3 fusion.60
  453.2 0.3 multiply_subtract_fusion
  453.6 1.0 maximum_convert_fusion
  454.5 2.3 gather_fusion.3
  456.8 2.2 gather_fusion.4
  459.0 1.9 select_bitcast_fusion
  460.9 1.9 fusion.31
  463.0 2.3 fusion.42
  465.3 1.8 copy.203
  467.1 0.9 convolution_multiply_fusion
  468.0 242.4 %psum.23 = f32[48,4,64]{0,2,1:T(8,128)S(1)} all-reduce(f32[48,4,64]{0,2,1:T(8,128)S(1)} %convolution_multiply_fusion), channel_id=1, replica_groups=mesh['gx'=4,'gy'=16,'sa'=4] {'gy','sa'}, use_global_device_ids=true, to_apply=%region_9.11 | all-reduce | flops 12288 | bytes 98304 | tf_op jit(solution)/shard_map/psum | solution.py:159
  710.4 0.9 fusion.46
  711.3 0.7 dynamic-slice_maximum_fusion
  712.0 0.9 fusion.47
  712.9 0.7 multiply_add_fusion.1
  713.6 0.8 copy.206
  714.4 0.8 copy.213
  715.4 1.7 fusion.28
  717.2 0.8 reshape.183
  717.9 11.9 %all_gather.11 = bf16[192,4,512]{2,0,1:T(8,128)(2,1)S(1)} all-gather(bf16[48,4,512]{2,0,1:T(8,128)(2,1)} %reshape.183), channel_id=1, replica_groups=mesh['gx'=4,'gy'=16,'sa'=4] {'gx'}, dimensions={0}, use_global_device_ids=true | all-gather | bytes 983040 | tf_op jit(solution)/shard_map/all_gather | solution.py:190
  729.8 4.5 fusion.7
  734.6 0.6 copy.217
  735.2 66.4 %reduce-scatter.5.cloned.1.call-done = f32[192,4,128]{2,0,1:T(8,128)} async-done(((f32[192,4,2048]{2,0,1:T(8,128)}), f32[192,4,128]{2,0,1:T(8,128)}) %reduce-scatter.5.cloned.1.call-update) | async-done | bytes 393232 | tf_op jit(solution)/shard_map/reduce_scatter | solution.py:194
  801.6 2.0 copy.216
  (72 shorter events, 2.0 us)
Async XLA Ops:
  7.2 722.7 %copy-start = (bf16[512,2048]{1,0:T(8,128)(2,1)S(1)}, bf16[512,2048]{1,0:T(8,128)(2,1)}, u32[]{:S(2)}) copy-start(bf16[512,2048]{1,0:T(8,128)(2,1)} %param.16) | copy-start | bytes 6291460
  7.2 13.5 %copy-start.13 = (bf16[2048]{0:T(1024)(128)(2,1)S(1)}, bf16[2048]{0:T(1024)(128)(2,1)}, u32[]{:S(2)}) copy-start(bf16[2048]{0:T(1024)(128)(2,1)} %param.13) | copy-start | bytes 12292
  7.2 59.8 %reduce-scatter.3.cloned.1.call-start = ((), (), s32[]{:S(2)}) async-start(), calls=%async_computation.2 | async-start | bytes 2457600 | tf_op jit(solution)/shard_map/reduce_scatter | solution.py:93
  20.7 3.8 copy-start.16
  24.5 3.5 copy-start.17
  33.0 77.2 %all-gather.2.cloned.1.call-start = ((), (), s32[]{:S(2)}) async-start(), calls=%async_computation.3 | async-start | bytes 3342336 | tf_op jit(solution)/shard_map/all_gather | solution.py:97
  68.8 646.6 %all-reduce.2.cloned.1.call-start = ((), (), s32[]{:S(2)}) async-start(), calls=%async_computation.4 | async-start | bytes 12582912 | tf_op jit(solution)/shard_map/psum | solution.py:159
  72.7 3.6 copy-start.18
  72.7 3.7 copy-start.14
  72.7 4.4 copy-start.15
  76.4 342.1 %copy-start.12 = (s32[8]{0:T(128)}, s32[8]{0:T(128)S(1)}, u32[]{:S(2)}) copy-start(s32[8]{0:T(128)S(1)} %get-tuple-element.22) | copy-start | bytes 100
  77.0 4.3 copy-start.3
  78.1 49.5 %copy-start.5 = (f32[48,4,64]{2,1,0:T(4,128)}, f32[48,4,64]{2,1,0:T(4,128)S(1)}, u32[]{:S(2)}) copy-start(f32[48,4,64]{2,1,0:T(4,128)S(1)} %get-tuple-element.36) | copy-start | bytes 147460
  143.2 1.7 copy-start.1
  143.2 2.6 copy-start.2
  159.6 258.8 %copy-start.8 = (f32[8,4,8,8]{3,1,2,0:T(4,128)}, f32[8,4,8,8]{3,1,2,0:T(4,128)S(1)}, u32[]{:S(2)}) copy-start(f32[8,4,8,8]{3,1,2,0:T(4,128)S(1)} %copy.193) | copy-start | bytes 24580
  413.3 5.1 copy-start.7
  418.5 2.8 copy-start.4
  427.8 0.9 copy-start.6
  427.9 373.7 %reduce-scatter.5.cloned.1.call-start = ((), (), s32[]{:S(2)}) async-start(), calls=%async_computation.5 | async-start | bytes 6684672 | tf_op jit(solution)/shard_map/reduce_scatter | solution.py:194
  452.0 1.3 copy-start.10
  452.0 1.3 copy-start.11
  453.2 7.7 copy-start.9
Sparse Core Ops, SparseCore 0:
  33.1 33.8 reduce-scatter.2
  69.4 40.7 all-gather.1
  428.0 200.9 all-reduce.1
  734.4 67.1 reduce-scatter.4
where the time goes:
time: 818 us; the launch traced here: 810 us
  blocking collectives  539 us (66%)
  waiting for transfers between devices  128 us (16%)
  local copies, waits for them, and re-layouts  52 us (6%)
  other arithmetic  50.9 us (6%)
  matrix products  25.6 us (3%)
  between operations  14.4 us (2%)
    pmax x1, blocking collectives, local(): top_all = lax.pmax(request_top, ('gy', 'sa'))  254 us
    psum x1, blocking collectives, local(): total_all, value_all = lax.psum((scaled_total, scaled_value), ('gy', 'sa'))  242 us
    reduce_scatter x1, waiting for transfers between devices, local(): lax.psum_scatter(projected_out, 'gy', scatter_dimension=2, tiled=True)  66.4 us
    reduce_scatter x1, waiting for transfers between devices, local(): lax.psum_scatter(jnp.concatenate([query_term, keyval_term], axis=-1), 'gx...  33.9 us
    all_gather x1, waiting for transfers between devices, local(): lax.all_gather(projected[..., :query_columns], 'gy', axis=2, tiled=True)  27.4 us
    all_gather x1, blocking collectives, local(): lax.all_gather(projected[..., query_columns:], 'gy', axis=2, tiled=True)  21.8 us
    unnamed x44, local copies, waits for them, and re-layouts  16.8 us
  transfers between devices with their start and end apart: 4, of which 3 were waited for; matrix products, arithmetic and copies ran while one was open for 5% of the time, Pallas kernels for 0%

commit v1 on v0

v1 whole, which is shorter than its diff:
```python
import jax
import jax.numpy as jnp
from jax import lax
from jax.experimental import pallas as pl
from jax.experimental.pallas import tpu as pltpu
from jax.sharding import PartitionSpec as P

D = 8192
QUERY_HEADS = 64
KEY_VALUE_HEADS = 8
HEAD = 128
GROUPS = 4
MEMBERS = 48
STEPS = 4
SLOTS = 8
PAGE = 128
PEERS = 64
ZN = 8
ROWS = GROUPS * MEMBERS

rope_base = 500000.0
norm_eps = 1e-05
neg_fill = -1e30
MESH = pl.DeviceIdType.MESH
f32 = jnp.float32
bf16 = jnp.bfloat16


def dot(a, b):
    return jnp.dot(a, b, preferred_element_type=f32)


def dot_nt(a, b):
    return lax.dot_general(a, b, (((1,), (1,)), ((), ())), preferred_element_type=f32)


def iota(shape, axis):
    return lax.broadcasted_iota(jnp.int32, shape, axis)


def lanes(index):
    return pl.ds(pl.multiple_of(index * HEAD, HEAD), HEAD)


def z_offset(k):
    return jnp.where(lax.rem(k, 2) == 1, (k + 1) // 2, lax.rem(ZN - k // 2, ZN))


def drain(ref, sem):
    pltpu.make_async_copy(ref, ref, sem).wait()


def kernel(
    x_ref, gain_ref, cos_ref, sin_ref, len_ref, own_ref, page_ref,
    wq_hbm, wkv_hbm, wo_hbm, k_hbm, v_hbm,
    out_ref, app_ref,
    wq, wkv, wo, kb, vb, xn, sqcol, sqs, ohs, ohr, live, perm, permt,
    qps, qpr, kps, kpr, qp, qsend, qrecv, kvs, appr, nkv, osend, orecv,
    lsend, lrecv, asend, arecv, acc, psend, precv, zsend, zrecv,
    load_sem, sq_s, sq_r, oh_s, oh_r, qp_s, qp_r, kp_s, kp_r, q_s, q_r,
    app_s, app_r, nk_s, nk_r, o_s, o_r, l_s, l_r, a_s, a_r,
    p_s, p_r, z_s, z_r, x_s, x_r,
):
    gx = lax.axis_index("gx")
    gy = lax.axis_index("gy")
    sa = lax.axis_index("sa")
    z = gy // 2
    core = lax.rem(gy, 2)
    me = gy * 4 + sa

    def remote(src, dst, ss, rs, dev):
        return pltpu.make_async_remote_copy(
            src_ref=src, dst_ref=dst, send_sem=ss, recv_sem=rs,
            device_id=dev, device_id_type=MESH,
        )

    loads = [
        pltpu.make_async_copy(a, b, load_sem.at[i])
        for i, (a, b) in enumerate(
            [(wq_hbm, wq), (wkv_hbm, wkv), (k_hbm, kb), (v_hbm, vb), (wo_hbm, wo)]
        )
    ]
    for c in loads:
        c.start()

    barrier = pltpu.get_barrier_semaphore()

    def greet(k, carry):
        peer = lax.rem(me + k, PEERS)
        pl.semaphore_signal(
            barrier, inc=1, device_id=(gx, peer // 4, lax.rem(peer, 4)), device_id_type=MESH
        )
        return carry

    lax.fori_loop(1, PEERS, greet, 0)

    def greet_y(k, carry):
        pl.semaphore_signal(
            barrier, inc=1,
            device_id=(lax.rem(gx + 1 + k // 4, GROUPS), gy, lax.rem(k, 4)),
            device_id_type=MESH,
        )
        return carry

    lax.fori_loop(0, 12, greet_y, 0)

    def square(i, carry):
        rows = pl.ds(pl.multiple_of(i * 16, 16), 16)
        xf = x_ref[rows, :].astype(f32)
        s = jnp.sum(xf * xf, axis=1, keepdims=True)
        sqcol[rows, :] = jnp.broadcast_to(s, (16, 128))
        return carry

    lax.fori_loop(0, ROWS // 16, square, 0)
    row128 = iota((128, 128), 0)
    lane128 = iota((128, 128), 1)
    eye = row128 == lane128
    r0 = jnp.sum(jnp.where(eye, sqcol[0:128, :], 0.0), axis=0, keepdims=True)
    r1 = jnp.sum(jnp.where(eye[0:64, :], sqcol[128:192, :], 0.0), axis=0, keepdims=True)
    sqs[gx, :, 0:128] = r0
    sqs[gx, :, 128:256] = r1

    row8 = iota((SLOTS, 128), 0)
    lane8 = iota((SLOTS, 128), 1)
    owner = jnp.zeros((SLOTS, 128), jnp.int32)
    for s in range(SLOTS):
        who = own_ref[s]
        page = page_ref[s]
        left = jnp.where(page >= 0, len_ref[who] - page * PAGE, 0)
        live[pl.ds(32 * s, 32), :] = (iota((32, 128), 1) < left).astype(f32)
        owner = jnp.where(row8 == s, who - gx * MEMBERS, owner)
    onehot = (lane8 == owner).astype(f32).astype(bf16)
    ohs[...] = onehot
    ohr[me] = onehot

    pl.semaphore_wait(barrier, PEERS - 1 + 12)

    for k in range(1, GROUPS):
        remote(
            sqs.at[gx], sqs.at[gx], sq_s.at[k - 1], sq_r.at[gx],
            (lax.rem(gx + k, GROUPS), gy, sa),
        ).start()

    def send_owner(k, carry):
        peer = lax.rem(me + k, PEERS)
        remote(ohs, ohr.at[me], oh_s, oh_r, (gx, peer // 4, lax.rem(peer, 4))).start()
        return carry

    lax.fori_loop(1, PEERS, send_owner, 0)

    pr = iota((256, 256), 0)
    pc = iota((256, 256), 1)
    want = ((pr >> 3) & 3) * 64 + (pr & 7) * 8 + (pr >> 5)
    perm[...] = (pc == want).astype(f32).astype(bf16)
    want = (pr & 7) * 32 + (pr >> 6) * 8 + ((pr >> 3) & 7)
    permt[...] = (pc == want).astype(f32).astype(bf16)
    qp[...] = jnp.zeros_like(qp)

    for k in range(1, GROUPS):
        src = lax.rem(gx + k, GROUPS)
        drain(sqs.at[src], sq_r.at[src])
    total = sqs[0] + sqs[1] + sqs[2] + sqs[3]
    t0 = jnp.broadcast_to(total[:, 0:128], (128, 128))
    t1 = jnp.broadcast_to(total[:, 128:256], (64, 128))
    c0 = jnp.sum(jnp.where(eye, t0, 0.0), axis=1, keepdims=True)
    c1 = jnp.sum(jnp.where(eye[0:64, :], t1, 0.0), axis=1, keepdims=True)
    sqcol[0:128, :] = jnp.broadcast_to(lax.rsqrt(c0 / D + norm_eps), (128, 128))
    sqcol[128:192, :] = jnp.broadcast_to(lax.rsqrt(c1 / D + norm_eps), (64, 128))

    def normalise(i, carry):
        rows = pl.ds(pl.multiple_of(i * 16, 16), 16)
        inv = sqcol[rows, 0:1]
        xf = x_ref[rows, :].astype(f32)
        xn[rows, :] = (xf * inv * gain_ref[...].astype(f32)).astype(bf16)
        return carry

    lax.fori_loop(0, ROWS // 16, normalise, 0)

    loads[0].wait()
    for n in range(2):
        part = dot(xn[...], wq[:, 256 * n : 256 * n + 256])
        for g in range(GROUPS):
            for h in range(2):
                qps[4 * g + 2 * n + h] = part[48 * g : 48 * g + 48, 128 * h : 128 * h + 128]

        def send_part(i, carry):
            g = lax.rem(gx + i // 2, GROUPS)
            head = 2 * n + lax.rem(i, 2)
            away = (g != gx) | (head != sa)

            @pl.when(away)
            def _():
                remote(
                    qps.at[4 * g + head], qpr.at[4 * gx + sa],
                    qp_s.at[4 * g + head], qp_r.at[4 * gx + sa], (g, gy, head),
                ).start()

            return carry

        lax.fori_loop(0, 8, send_part, 0)
    loads[1].wait()
    part = dot(xn[...], wkv[...])
    for g in range(GROUPS):
        kps[g] = part[48 * g : 48 * g + 48, :]
    for k in range(1, GROUPS):
        g = lax.rem(gx + k, GROUPS)
        remote(kps.at[g], kpr.at[gx], kp_s.at[g], kp_r.at[gx], (g, gy, sa)).start()
    qpr[4 * gx + sa] = qps[4 * gx + sa]
    kpr[gx] = kps[gx]

    def rotate(value, cos, sin):
        return value * cos + pltpu.roll(value, HEAD // 2, 1) * sin

    drain(ohr.at[pl.ds(0, PEERS - 1)], oh_r)

    def wait_part(i, carry):
        @pl.when(i != 4 * gx + sa)
        def _():
            drain(qpr.at[i], qp_r.at[i])

        return carry

    lax.fori_loop(0, 16, wait_part, 0)
    for t in range(STEPS):
        q = qpr[t] + qpr[4 + t] + qpr[8 + t] + qpr[12 + t]
        q = q.astype(bf16).astype(f32)
        at = slice(HEAD * t, HEAD * t + HEAD)
        qp[0:MEMBERS, at] = rotate(q, cos_ref[:, at], sin_ref[:, at]).astype(bf16)

    def send_query(k, carry):
        zd = lax.rem(z + z_offset(k), ZN)
        block = pl.ds(zd * 8, 8)
        pick = ohr[block].astype(f32).reshape(64, 128).astype(bf16)
        qsend[block] = dot(pick, qp[...]).reshape(8, SLOTS, 512).astype(bf16)

        def one(i, c):
            peer = zd * 8 + i

            @pl.when(peer != me)
            def _():
                remote(
                    qsend.at[peer], qrecv.at[me], q_s, q_r.at[z],
                    (gx, peer // 4, lax.rem(peer, 4)),
                ).start()

            return c

        return lax.fori_loop(0, 8, one, carry)

    lax.fori_loop(0, ZN, send_query, 0)
    qrecv[me] = qsend[me]

    def wait_kv(i, carry):
        @pl.when(i != gx)
        def _():
            drain(kpr.at[i], kp_r.at[i])

        return carry

    lax.fori_loop(0, GROUPS, wait_kv, 0)
    kv = (kpr[0] + kpr[1] + kpr[2] + kpr[3]).astype(bf16).astype(f32)
    turned = rotate(kv, cos_ref[:, lanes(sa)], sin_ref[:, lanes(sa)])
    kv = jnp.where(gy < KEY_VALUE_HEADS, turned, kv).astype(bf16)
    kvs[...] = kv
    appr[sa] = kv
    which = gy // 8
    target = lax.rem(gy, 8) * 2

    def send_new(i, carry):
        dgy = target + i // 4
        dsa = lax.rem(i, 4)
        away = (dgy != gy) | (dsa != sa)

        @pl.when(away)
        def _():
            remote(
                kvs, nkv.at[4 * which + sa], nk_s.at[i], nk_r.at[4 * which + sa],
                (gx, dgy, dsa),
            ).start()

        @pl.when(jnp.logical_not(away))
        def _():
            nkv[4 * which + sa] = kvs[...]

        return carry

    lax.fori_loop(0, 8, send_new, 0)
    for k in range(1, 4):
        remote(
            kvs, appr.at[sa], app_s.at[k - 1], app_r.at[sa], (gx, gy, lax.rem(sa + k, 4))
        ).start()

    loads[2].wait()
    loads[3].wait()
    scale = HEAD ** (-0.5)

    def attend(k, carry):
        j = lax.rem(z + ZN - z_offset(k), ZN)
        block = pl.ds(j * 8, 8)

        @pl.when(j == z)
        def _():
            drain(qrecv.at[pl.ds(0, 7)], q_r.at[j])

        @pl.when(j != z)
        def _():
            drain(qrecv.at[pl.ds(0, 8)], q_r.at[j])

        got = [
            qrecv[block, :, HEAD * t : HEAD * t + HEAD].astype(f32).reshape(64, HEAD)
            for t in range(STEPS)
        ]
        rows = dot(perm[...], jnp.concatenate(got, axis=0).astype(bf16)).astype(bf16)
        score = jnp.concatenate(
            [dot_nt(rows[32 * s : 32 * s + 32], kb[s, :, lanes(j)]) for s in range(SLOTS)], axis=0
        )
        mask = live[...]
        score = jnp.where(mask > 0.0, score * scale, neg_fill)
        top = jnp.max(score, axis=1, keepdims=True)
        weight = jnp.exp(score - top) * mask
        mass = jnp.sum(weight, axis=1, keepdims=True)
        weight = weight.astype(bf16)
        value = jnp.concatenate(
            [dot(weight[32 * s : 32 * s + 32], vb[s, :, lanes(j)]) for s in range(SLOTS)], axis=0
        )
        held = mass > 0.0
        mass = jnp.where(held, mass, 1.0)
        lse = jnp.where(held, top + jnp.log(mass), neg_fill)
        back = dot(permt[...], (value / mass).astype(bf16))
        for t in range(STEPS):
            osend[block, :, HEAD * t : HEAD * t + HEAD] = (
                back[64 * t : 64 * t + 64].reshape(8, SLOTS, HEAD).astype(bf16)
            )
        packed = jnp.zeros((8, 128), f32)
        for i in range(32):
            column = jnp.broadcast_to(lse[8 * i : 8 * i + 8], (8, 128))
            packed = jnp.where(lane8 == i, column, packed)
        for i in range(8):
            lsend[8 * j + i] = packed[i : i + 1]

        def one(i, c):
            peer = j * 8 + i

            @pl.when(peer != me)
            def _():
                dev = (gx, peer // 4, lax.rem(peer, 4))
                remote(osend.at[peer], orecv.at[me], o_s, o_r, dev).start()
                remote(lsend.at[peer], lrecv.at[me], l_s, l_r, dev).start()

            return c

        return lax.fori_loop(0, 8, one, carry)

    lax.fori_loop(0, ZN, attend, 0)
    orecv[me] = osend[me]
    lrecv[me] = lsend[me]

    def wait_new(i, carry):
        sgy = gy // 2 + 8 * (i // 4)

        @pl.when((sgy != gy) | (lax.rem(i, 4) != sa))
        def _():
            drain(nkv.at[i], nk_r.at[i])

        return carry

    lax.fori_loop(0, 8, wait_new, 0)
    fresh = {}
    for u in range(STEPS):
        q = qp[0:MEMBERS, HEAD * u : HEAD * u + HEAD].astype(f32)
        for v in range(u + 1):
            prod = q * nkv[v].astype(f32)
            fresh[u, v] = jnp.sum(prod, axis=1, keepdims=True) * scale
    for k in range(1, 4):
        src = lax.rem(sa + k, 4)
        drain(appr.at[src], app_r.at[src])
    for t in range(STEPS):
        app_ref[:, HEAD * t : HEAD * t + HEAD] = appr[t]

    held_by = dot_nt(
        (iota((MEMBERS, 128), 0) == iota((MEMBERS, 128), 1)).astype(f32).astype(bf16),
        ohr[...].astype(f32).reshape(512, 128).astype(bf16),
    )
    mine = held_by > 0.5

    drain(lrecv.at[pl.ds(0, PEERS - 1)], l_r)
    spread = jnp.broadcast_to(lrecv[...], (PEERS, SLOTS, 128)).reshape(512, 128)
    slot_of = iota((512, 128), 0) & 7
    lane512 = iota((512, 128), 1)
    table = jnp.zeros((512, 128), f32)
    for t in range(STEPS):
        column = jnp.sum(
            jnp.where(lane512 == slot_of * 4 + t, spread, 0.0), axis=1, keepdims=True
        )
        table = jnp.where(lane512 == t, column, table)
    table = jnp.transpose(table)
    drain(orecv.at[pl.ds(0, PEERS - 1)], o_r)
    for t in range(STEPS):
        lse = jnp.where(mine, table[t : t + 1, :], neg_fill)
        top = jnp.max(lse, axis=1, keepdims=True)
        for v in range(t + 1):
            top = jnp.maximum(top, fresh[t, v])
        weight = jnp.exp(lse - top)
        mass = jnp.sum(weight, axis=1, keepdims=True)
        high = weight.astype(bf16)
        low = (weight - high.astype(f32)).astype(bf16)
        pages = (
            orecv[:, :, HEAD * t : HEAD * t + HEAD].astype(f32).reshape(512, HEAD).astype(bf16)
        )
        value = dot(high, pages) + dot(low, pages)
        for v in range(t + 1):
            w = jnp.exp(fresh[t, v] - top)
            mass = mass + w
            value = value + w * nkv[4 + v].astype(f32)
        asend[t] = (value / mass).astype(bf16)

    def send_head(i, carry):
        g = lax.rem(gx + i // 4, GROUPS)
        t = lax.rem(sa + lax.rem(i, 4), 4)
        away = (g != gx) | (t != sa)

        @pl.when(away)
        def _():
            remote(
                asend.at[t], arecv.at[gx, :, lanes(sa)], a_s.at[4 * g + t],
                a_r.at[4 * gx + sa], (g, gy, t),
            ).start()

        @pl.when(jnp.logical_not(away))
        def _():
            arecv[gx, :, lanes(sa)] = asend[sa]

        return carry

    lax.fori_loop(0, 16, send_head, 0)
    loads[4].wait()

    def wait_head(i, carry):
        @pl.when(i != 4 * gx + sa)
        def _():
            drain(arecv.at[i // 4, :, lanes(lax.rem(i, 4))], a_r.at[i])

        return carry

    lax.fori_loop(0, 16, wait_head, 0)
    partner = (gx, gy + 1 - 2 * core, sa)
    first = core == 0

    def product(k, carry):
        zd = lax.rem(z + z_offset(ZN - 1 - k), ZN)
        part = dot(
            arecv[...].reshape(ROWS, 512), wo[:, pl.ds(pl.multiple_of(zd * 256, 256), 256)]
        )
        a, b = part[:, 0:128], part[:, 128:256]
        acc[zd] = jnp.where(first, a, b)
        psend[zd] = jnp.where(first, b, a)
        remote(psend.at[zd], precv.at[zd], p_s.at[zd], p_r.at[zd], partner).start()
        return carry

    lax.fori_loop(0, ZN, product, 0)

    def chip_sum(k, carry):
        zd = lax.rem(z + z_offset(ZN - 1 - k), ZN)
        drain(precv.at[zd], p_r.at[zd])
        both = acc[zd] + precv[zd]

        @pl.when(zd != z)
        def _():
            zsend[zd] = both.astype(bf16)
            remote(
                zsend.at[zd], zrecv.at[z], z_s.at[zd], z_r.at[z], (gx, 2 * zd + core, sa)
            ).start()

        @pl.when(zd == z)
        def _():
            acc[zd] = both

        return carry

    lax.fori_loop(0, ZN, chip_sum, 0)

    def gather_sum(k, carry):
        src = lax.rem(z + k, ZN)
        drain(zrecv.at[src], z_r.at[src])
        acc[z] += zrecv[src].astype(f32)
        return carry

    lax.fori_loop(1, ZN, gather_sum, 0)
    out_ref[sa] = acc[z]
    for k in range(1, 4):
        remote(
            out_ref.at[sa], out_ref.at[sa], x_s.at[k - 1], x_r.at[sa],
            (gx, gy, lax.rem(sa + k, 4)),
        ).start()
    for k in range(1, 4):
        src = lax.rem(sa + k, 4)
        drain(out_ref.at[src], x_r.at[src])

    for k in range(3):
        drain(sqs.at[gx], sq_s.at[k])
        drain(kvs, app_s.at[k])
        drain(out_ref.at[sa], x_s.at[k])
    drain(ohr.at[pl.ds(0, PEERS - 1)], oh_s)
    drain(qsend.at[pl.ds(0, PEERS - 1)], q_s)
    drain(osend.at[pl.ds(0, PEERS - 1)], o_s)
    drain(lsend.at[pl.ds(0, PEERS - 1)], l_s)

    def sent16(i, carry):
        @pl.when(i != 4 * gx + sa)
        def _():
            drain(qps.at[i], qp_s.at[i])
            drain(asend.at[0], a_s.at[i])

        return carry

    lax.fori_loop(0, 16, sent16, 0)

    def sent8(i, carry):
        drain(psend.at[i], p_s.at[i])

        @pl.when((target + i // 4 != gy) | (lax.rem(i, 4) != sa))
        def _():
            drain(kvs, nk_s.at[i])

        @pl.when(i != z)
        def _():
            drain(zsend.at[i], z_s.at[i])

        return carry

    lax.fori_loop(0, 8, sent8, 0)

    def sent4(i, carry):
        @pl.when(i != gx)
        def _():
            drain(kps.at[i], kp_s.at[i])

        return carry

    lax.fori_loop(0, GROUPS, sent4, 0)


def local(
    tokens, norm_gain, w_query, w_keyval, w_out,
    paged_key_cache, paged_value_cache, lengths, slot_owner, slot_page_number,
):
    gx = lax.axis_index("gx")
    sa = lax.axis_index("sa")
    x = lax.dynamic_index_in_dim(tokens, sa, 1, keepdims=False)
    group_lengths = lax.dynamic_slice_in_dim(lengths, gx * MEMBERS, MEMBERS)
    lane = jnp.arange(STEPS * HEAD, dtype=jnp.int32)
    exponent = (lane % (HEAD // 2)).astype(f32) * (-2.0 / HEAD)
    inverse_freq = jnp.power(f32(rope_base), exponent)
    angles = (group_lengths[:, None] + lane[None, :] // HEAD).astype(f32) * inverse_freq[None, :]
    cosine = jnp.cos(angles)
    sine = jnp.sin(angles)
    sine = jnp.where(lane[None, :] % HEAD < HEAD // 2, -sine, sine)

    vmem = pl.BlockSpec(memory_space=pltpu.VMEM)
    smem = pl.BlockSpec(memory_space=pltpu.SMEM)
    hbm = pl.BlockSpec(memory_space=pl.ANY)
    dma = pltpu.SemaphoreType.DMA
    V = pltpu.VMEM
    mixed, appended = pl.pallas_call(
        kernel,
        out_shape=(
            jax.ShapeDtypeStruct((STEPS, ROWS, HEAD), f32),
            jax.ShapeDtypeStruct((MEMBERS, STEPS * HEAD), bf16),
        ),
        in_specs=[vmem] * 4 + [smem] * 3 + [hbm] * 5,
        out_specs=(vmem, vmem),
        scratch_shapes=[
            V((2048, 512), bf16), V((2048, 128), bf16), V((512, 2048), bf16),
            V((SLOTS, PAGE, 1024), bf16), V((SLOTS, PAGE, 1024), bf16),
            V((ROWS, 2048), bf16), V((ROWS, 128), f32), V((GROUPS, 1, 256), f32),
            V((SLOTS, 128), bf16), V((PEERS, SLOTS, 128), bf16), V((256, 128), f32),
            V((256, 256), bf16), V((256, 256), bf16),
            V((16, MEMBERS, HEAD), f32), V((16, MEMBERS, HEAD), f32),
            V((GROUPS, MEMBERS, HEAD), f32), V((GROUPS, MEMBERS, HEAD), f32),
            V((128, 512), bf16),
            V((PEERS, SLOTS, 512), bf16), V((PEERS, SLOTS, 512), bf16),
            V((MEMBERS, HEAD), bf16), V((4, MEMBERS, HEAD), bf16), V((8, MEMBERS, HEAD), bf16),
            V((PEERS, SLOTS, 512), bf16), V((PEERS, SLOTS, 512), bf16),
            V((PEERS, 1, 128), f32), V((PEERS, 1, 128), f32),
            V((STEPS, MEMBERS, HEAD), bf16), V((GROUPS, MEMBERS, 512), bf16),
            V((ZN, ROWS, HEAD), f32), V((ZN, ROWS, HEAD), f32), V((ZN, ROWS, HEAD), f32),
            V((ZN, ROWS, HEAD), bf16), V((ZN, ROWS, HEAD), bf16),
            dma((5,)), dma((3,)), dma((4,)), dma, dma, dma((16,)), dma((16,)), dma((4,)),
            dma((4,)), dma, dma((8,)), dma((3,)), dma((4,)), dma((8,)), dma((8,)),
            dma, dma, dma, dma, dma((16,)), dma((16,)), dma((8,)), dma((8,)), dma((8,)),
            dma((8,)), dma((3,)), dma((4,)),
        ],
        compiler_params=pltpu.CompilerParams(
            collective_id=0, has_side_effects=True, vmem_limit_bytes=60 * 1024 * 1024
        ),
        name="paged_attention_layer",
    )(
        x, norm_gain.reshape(1, -1), cosine, sine, lengths, slot_owner, slot_page_number,
        w_query, w_keyval, w_out, paged_key_cache, paged_value_cache,
    )
    return (
        jnp.transpose(mixed, (1, 0, 2)),
        appended.reshape(MEMBERS, STEPS, HEAD),
    )


def solution(mesh):
    in_specs = (
        P(None, None, "gx"),
        P("gx"),
        P("gx", "gy"),
        P("gx", "gy"),
        P("gy", "gx"),
        P(("gx", "gy", "sa"), None, None),
        P(("gx", "gy", "sa"), None, None),
        P(),
        P(("gx", "gy", "sa")),
        P(("gx", "gy", "sa")),
    )
    out_specs = (P(None, None, ("gx", "gy")), P("gx", None, "gy"))
    return jax.shard_map(local, mesh=mesh, in_specs=in_specs, out_specs=out_specs, check_vma=False)
```

time: 818 us -> 94.2 us (0.12)
  blocking collectives: 539 us -> 0 us
  waiting for transfers between devices: 128 us -> 0 us
  Pallas kernels: 0 us -> 82.8 us
  other arithmetic: 50.9 us -> 1.13 us
  local copies, waits for them, and re-layouts: 52 us -> 9 us
  matrix products: 25.6 us -> 0 us
  between operations: 14.4 us -> 0.67 us
    pmax x1 -> x0, blocking collectives: 254 us -> none  [local(): top_all = lax.pmax(request_top, ('gy', 'sa'))]
    psum x2 -> x0, blocking collectives: 252 us -> none  [the longest x1 242 us: local(): total_all, value_all = lax.psum((scaled_total, scaled_value), ('gy', 'sa'))]
    reduce_scatter x2 -> x0, waiting for transfers between devices: 100 us -> none  [the longest x1 66.4 us: local(): lax.psum_scatter(projected_out, 'gy', scatter_dimension=2, tiled=True)]
    pallas_call x0 -> x1, Pallas kernels: none -> 82.8 us  [local(): pl.pallas_call(kernel, out_shape=(jax.ShapeDtypeStruct((STEPS, ROWS, HEAD...]
    all_gather x2 -> x0, blocking collectives: 33.7 us -> none  [the longest x1 21.8 us: local(): lax.all_gather(projected[..., query_columns:], 'gy', axis=2, tiled=True)]
    all_gather x1 -> x0, waiting for transfers between devices: 27.4 us -> none  [local(): lax.all_gather(projected[..., :query_columns], 'gy', axis=2, tiled=True)]
    dot_general x9 -> x0, matrix products: 25.6 us -> none  [the longest x1 4.45 us: local(): jnp.einsum('ruk,kc->ruc', lax.all_gather(attended, 'gx', axis=0, tiled=Tr...]
    another operation x1 -> x0, other arithmetic: 15.6 us -> none
  transfers between devices with their start and end apart: 4 -> 0, of which waited for: 3 -> 0; matrix products, arithmetic and copies ran while one was open for 5% -> 0% of each run, Pallas kernels for 0% -> 0%
where the time goes in v1:
time: 94.2 us; the launch traced here: 93.6 us
  Pallas kernels  82.8 us (88%)
  local copies, waits for them, and re-layouts  9 us (10%)
  other arithmetic  1.13 us (1%)
    pallas_call x1, Pallas kernels, local(): pl.pallas_call(kernel, out_shape=(jax.ShapeDtypeStruct((STEPS, ROWS, HEAD...  82.8 us
    unnamed x8, local copies, waits for them, and re-layouts  5.23 us

profile of v1, /device:TPU:1, one launch (start us, length us, event | category | flops | bytes accessed | tf_op | source)
XLA Modules:
  0.0 93.6 jit_solution(1068935230379421742)
XLA Ops:
  0.6 0.0 copy-start
  0.6 1.9 %copy-done = bf16[192,4,2048]{2,1,0:T(4,128)(2,1)S(1)} copy-done((bf16[192,4,2048]{2,1,0:T(4,128)(2,1)S(1)}, bf16[192,4,2048]{2,1,0:T(4,128)(2,1)}, u32[]{:S(2)}) %copy-start) | copy-done | bytes 3145752
  2.5 0.0 copy-start.1
  2.5 0.0 copy-start.2
  2.5 1.7 %constant_dynamic-slice_fusion = bf16[192,1,2048]{2,1,0:T(2,128)(2,1)S(1)} fusion(bf16[192,4,2048]{2,1,0:T(4,128)(2,1)S(1)} %copy-done, s32[]{:T(128)S(6)} %select_n.43), kind=kLoop, calls=%fused_computation.24 | loop fusion | bytes 1572868 | tf_op jit(solution)/shard_map/jit(dynamic_index_in_dim)/dynamic_slice | solution.py:549
  4.2 1.3 %copy.17 = bf16[192,1,2048]{2,0,1:T(8,128)(2,1)} copy(bf16[192,1,2048]{2,1,0:T(2,128)(2,1)S(1)} %constant_dynamic-slice_fusion) | data formatting | bytes 1572864
  5.5 0.0 copy-done.1
  5.5 0.6 reshape.77.gain_ref
  6.2 0.0 copy-done.2
  6.2 0.1 dynamic_slice.8
  6.2 1.1 %negate_select_fusion = (f32[48,512]{1,0:T(8,128)}, f32[48,512]{1,0:T(8,128)}) fusion(f32[512]{0:T(512)S(1)} %fusion.7, s32[512]{0:T(512)S(1)} %add_select_fusion.1, s32[48]{0:T(128)S(1)} %dynamic_slice.8, pred[512]{0:T(512)(128)(4,1)S(1)} %fusion.8), kind=kLoop, calls=%fused_computation.1 | loop fusion | flops 122880 | bytes 201408 | tf_op jit(solution)/shard_map/jit(_where)/select_n | solution.py:557
  7.4 82.8 %paged_attention_layer.1 = (f32[4,192,128]{2,1,0:T(8,128)}, bf16[48,512]{1,0:T(8,128)(2,1)}) custom-call(bf16[192,2048]{1,0:T(8,128)(2,1)} %bitcast.4, bf16[1,2048]{1,0:T(2,128)(2,1)} %reshape.77.gain_ref, f32[48,512]{1,0:T(8,128)} %get-tuple-element.11.cos_ref, f32[48,512]{1,0:T(8,128)} %get-tuple-element.10.sin_ref, s32[192]{0:T(256)} %len_ref.1, ...), custom_call_target="tpu_custom_call" | custom-call | tf_op jit(solution)/shard_map/paged_attention_layer/pallas_call | solution.py:564
  90.2 2.0 %copy.14 = f32[192,4,128]{2,1,0:T(4,128)} copy(f32[192,4,128]{2,0,1:T(8,128)} %bitcast.5) | data formatting | bytes 786432
  92.2 1.4 %reshape.78 = bf16[48,4,128]{2,1,0:T(4,128)(2,1)} reshape(bf16[48,512]{1,0:T(8,128)(2,1)} %get-tuple-element.5) | data formatting | bytes 98304 | tf_op jit(solution)/shard_map/reshape | solution.py:603
  (3 shorter events, 0.0 us)
Async XLA Ops:
  0.6 1.9 %copy-start = (bf16[192,4,2048]{2,1,0:T(4,128)(2,1)S(1)}, bf16[192,4,2048]{2,1,0:T(4,128)(2,1)}, u32[]{:S(2)}) copy-start(bf16[192,4,2048]{2,1,0:T(4,128)(2,1)} %param.10) | copy-start | bytes 9437188
  2.5 3.0 %copy-start.1 = (bf16[2048]{0:T(1024)(128)(2,1)S(1)}, bf16[2048]{0:T(1024)(128)(2,1)}, u32[]{:S(2)}) copy-start(bf16[2048]{0:T(1024)(128)(2,1)} %param.11) | copy-start | bytes 12292
  2.5 3.6 %copy-start.2 = (s32[192]{0:T(256)S(1)}, s32[192]{0:T(256)}, u32[]{:S(2)}) copy-start(s32[192]{0:T(256)} %len_ref.1) | copy-start | bytes 2308

commit v2 on v1

--- a/solution.py
+++ b/solution.py
@@ -53,7 +53,7 @@
 def kernel(
     x_ref, gain_ref, cos_ref, sin_ref, len_ref, own_ref, page_ref,
     wq_hbm, wkv_hbm, wo_hbm, k_hbm, v_hbm,
-    out_ref, app_ref,
+    out_ref, app_ref, xrecv, gain_row,
     wq, wkv, wo, kb, vb, xn, sqcol, sqs, ohs, ohr, live, perm, permt,
     qps, qpr, kps, kpr, qp, qsend, qrecv, kvs, appr, nkv, osend, orecv,
     lsend, lrecv, asend, arecv, acc, psend, precv, zsend, zrecv,
@@ -104,6 +104,9 @@
 
     lax.fori_loop(0, 12, greet_y, 0)
 
+    gain = gain_ref[...].astype(f32)
+    gain_row[...] = jnp.concatenate([gain[c : c + 1] for c in range(16)], axis=1)
+
     def square(i, carry):
         rows = pl.ds(pl.multiple_of(i * 16, 16), 16)
         xf = x_ref[rows, :].astype(f32)
@@ -171,7 +174,7 @@
         rows = pl.ds(pl.multiple_of(i * 16, 16), 16)
         inv = sqcol[rows, 0:1]
         xf = x_ref[rows, :].astype(f32)
-        xn[rows, :] = (xf * inv * gain_ref[...].astype(f32)).astype(bf16)
+        xn[rows, :] = (xf * inv * gain_row[...]).astype(bf16)
         return carry
 
     lax.fori_loop(0, ROWS // 16, normalise, 0)
@@ -374,8 +377,11 @@
     for k in range(1, 4):
         src = lax.rem(sa + k, 4)
         drain(appr.at[src], app_r.at[src])
-    for t in range(STEPS):
-        app_ref[:, HEAD * t : HEAD * t + HEAD] = appr[t]
+    ar = iota((ROWS, ROWS), 0)
+    weave = iota((ROWS, ROWS), 1) == (ar & 3) * MEMBERS + (ar >> 2)
+    app_ref[...] = dot(
+        weave.astype(f32).astype(bf16), appr[...].reshape(STEPS * MEMBERS, HEAD)
+    ).astype(bf16)
 
     held_by = dot_nt(
         (iota((MEMBERS, 128), 0) == iota((MEMBERS, 128), 1)).astype(f32).astype(bf16),
@@ -455,9 +461,12 @@
         acc[zd] = jnp.where(first, a, b)
         psend[zd] = jnp.where(first, b, a)
         remote(psend.at[zd], precv.at[zd], p_s.at[zd], p_r.at[zd], partner).start()
-        return carry
-
-    lax.fori_loop(0, ZN, product, 0)
+
+        @pl.when(k >= 2)
+        def _():
+            chip_sum(k - 2, 0)
+
+        return carry
 
     def chip_sum(k, carry):
         zd = lax.rem(z + z_offset(ZN - 1 - k), ZN)
@@ -477,7 +486,8 @@
 
         return carry
 
-    lax.fori_loop(0, ZN, chip_sum, 0)
+    lax.fori_loop(0, ZN, product, 0)
+    lax.fori_loop(ZN - 2, ZN, chip_sum, 0)
 
     def gather_sum(k, carry):
         src = lax.rem(z + k, ZN)
@@ -486,20 +496,22 @@
         return carry
 
     lax.fori_loop(1, ZN, gather_sum, 0)
-    out_ref[sa] = acc[z]
+    xrecv[sa] = acc[z].astype(bf16)
     for k in range(1, 4):
         remote(
-            out_ref.at[sa], out_ref.at[sa], x_s.at[k - 1], x_r.at[sa],
+            xrecv.at[sa], xrecv.at[sa], x_s.at[k - 1], x_r.at[sa],
             (gx, gy, lax.rem(sa + k, 4)),
         ).start()
     for k in range(1, 4):
         src = lax.rem(sa + k, 4)
-        drain(out_ref.at[src], x_r.at[src])
+        drain(xrecv.at[src], x_r.at[src])
+    for t in range(STEPS):
+        out_ref[pl.ds(t, ROWS, stride=STEPS), :] = xrecv[t].astype(f32)
 
     for k in range(3):
         drain(sqs.at[gx], sq_s.at[k])
         drain(kvs, app_s.at[k])
-        drain(out_ref.at[sa], x_s.at[k])
+        drain(xrecv.at[sa], x_s.at[k])
     drain(ohr.at[pl.ds(0, PEERS - 1)], oh_s)
     drain(qsend.at[pl.ds(0, PEERS - 1)], q_s)
     drain(osend.at[pl.ds(0, PEERS - 1)], o_s)
@@ -564,12 +576,13 @@
     mixed, appended = pl.pallas_call(
         kernel,
         out_shape=(
-            jax.ShapeDtypeStruct((STEPS, ROWS, HEAD), f32),
-            jax.ShapeDtypeStruct((MEMBERS, STEPS * HEAD), bf16),
+            jax.ShapeDtypeStruct((STEPS * ROWS, HEAD), f32),
+            jax.ShapeDtypeStruct((MEMBERS * STEPS, HEAD), bf16),
         ),
         in_specs=[vmem] * 4 + [smem] * 3 + [hbm] * 5,
         out_specs=(vmem, vmem),
         scratch_shapes=[
+            V((STEPS, ROWS, HEAD), bf16), V((1, 2048), f32),
             V((2048, 512), bf16), V((2048, 128), bf16), V((512, 2048), bf16),
             V((SLOTS, PAGE, 1024), bf16), V((SLOTS, PAGE, 1024), bf16),
             V((ROWS, 2048), bf16), V((ROWS, 128), f32), V((GROUPS, 1, 256), f32),
@@ -595,11 +608,11 @@
         ),
         name="paged_attention_layer",
     )(
-        x, norm_gain.reshape(1, -1), cosine, sine, lengths, slot_owner, slot_page_number,
+        x, norm_gain.reshape(16, 128), cosine, sine, lengths, slot_owner, slot_page_number,
         w_query, w_keyval, w_out, paged_key_cache, paged_value_cache,
     )
     return (
-        jnp.transpose(mixed, (1, 0, 2)),
+        mixed.reshape(ROWS, STEPS, HEAD),
         appended.reshape(MEMBERS, STEPS, HEAD),
     )
 

time: 94.2 us -> 91.5 us (0.971)
  Pallas kernels: 82.8 us -> 81.3 us
    reshape x2 -> x0, local copies, waits for them, and re-layouts: 2.04 us -> none  [the longest x1 1.43 us: local(): appended.reshape(MEMBERS, STEPS, HEAD)]
    pallas_call x1, Pallas kernels: 82.8 us -> 81.3 us  [local(): pl.pallas_call(kernel, out_shape=(jax.ShapeDtypeStruct((STEPS * ROWS, HEA...]
    unnamed x8 -> x7, local copies, waits for them, and re-layouts: 5.23 us -> 6.43 us
where the time goes in v2:
time: 91.5 us; the launch traced here: 91.3 us
  Pallas kernels  81.3 us (89%)
  local copies, waits for them, and re-layouts  8.16 us (9%)
  other arithmetic  1.13 us (1%)
    pallas_call x1, Pallas kernels, local(): pl.pallas_call(kernel, out_shape=(jax.ShapeDtypeStruct((STEPS * ROWS, HEA...  81.3 us
    unnamed x7, local copies, waits for them, and re-layouts  6.43 us

profile of v2, /device:TPU:1, one launch (start us, length us, event | category | flops | bytes accessed | tf_op | source)
XLA Modules:
  0.0 91.3 jit_solution(1919698895446860489)
XLA Ops:
  0.6 0.0 copy-start
  0.6 1.9 %copy-done = bf16[192,4,2048]{2,1,0:T(4,128)(2,1)S(1)} copy-done((bf16[192,4,2048]{2,1,0:T(4,128)(2,1)S(1)}, bf16[192,4,2048]{2,1,0:T(4,128)(2,1)}, u32[]{:S(2)}) %copy-start) | copy-done | bytes 3145752
  2.5 0.0 copy-start.1
  2.5 1.7 %constant_dynamic-slice_fusion = bf16[192,1,2048]{2,1,0:T(2,128)(2,1)S(1)} fusion(bf16[192,4,2048]{2,1,0:T(4,128)(2,1)S(1)} %copy-done, s32[]{:T(128)S(6)} %select_n.43), kind=kLoop, calls=%fused_computation.24 | loop fusion | bytes 1572868 | tf_op jit(solution)/shard_map/jit(dynamic_index_in_dim)/dynamic_slice | solution.py:561
  4.2 1.3 %copy.15 = bf16[192,1,2048]{2,0,1:T(8,128)(2,1)} copy(bf16[192,1,2048]{2,1,0:T(2,128)(2,1)S(1)} %constant_dynamic-slice_fusion) | data formatting | bytes 1572864
  5.5 0.0 copy-done.1
  5.6 0.1 dynamic_slice.8
  5.6 1.1 %negate_select_fusion = (f32[48,512]{1,0:T(8,128)}, f32[48,512]{1,0:T(8,128)}) fusion(f32[512]{0:T(512)S(1)} %fusion.7, s32[512]{0:T(512)S(1)} %add_select_fusion.1, s32[48]{0:T(128)S(1)} %dynamic_slice.8, pred[512]{0:T(512)(128)(4,1)S(1)} %fusion.8), kind=kLoop, calls=%fused_computation.1 | loop fusion | flops 122880 | bytes 201408 | tf_op jit(solution)/shard_map/jit(_where)/select_n | solution.py:569
  6.8 81.3 %paged_attention_layer.1 = (f32[768,128]{1,0:T(8,128)}, bf16[192,128]{1,0:T(8,128)(2,1)}) custom-call(bf16[192,2048]{1,0:T(8,128)(2,1)} %bitcast.6, bf16[16,128]{1,0:T(8,128)(2,1)} %bitcast.9, f32[48,512]{1,0:T(8,128)} %get-tuple-element.7.cos_ref, f32[48,512]{1,0:T(8,128)} %get-tuple-element.6.sin_ref, s32[192]{0:T(256)} %len_ref.1, s32[8]{0:T(128)} %own_ref.1, ...), custom_call_target="tpu_custom_call" | custom-call | tf_op jit(solution)/shard_map/paged_attention_layer/pallas_call | solution.py:576
  88.1 1.8 %copy.18 = f32[192,4,128]{2,1,0:T(4,128)} copy(f32[192,4,128]{2,1,0:T(4,128)} %bitcast.7) | data formatting | bytes 786432
  89.9 1.4 %copy.19 = bf16[48,4,128]{2,1,0:T(4,128)(2,1)} copy(bf16[48,4,128]{2,1,0:T(4,128)(2,1)} %bitcast.8) | data formatting | bytes 98304
  (3 shorter events, 0.0 us)
Async XLA Ops:
  0.6 1.9 %copy-start = (bf16[192,4,2048]{2,1,0:T(4,128)(2,1)S(1)}, bf16[192,4,2048]{2,1,0:T(4,128)(2,1)}, u32[]{:S(2)}) copy-start(bf16[192,4,2048]{2,1,0:T(4,128)(2,1)} %param.10) | copy-start | bytes 9437188
  2.5 3.0 %copy-start.1 = (s32[192]{0:T(256)S(1)}, s32[192]{0:T(256)}, u32[]{:S(2)}) copy-start(s32[192]{0:T(256)} %len_ref.1) | copy-start | bytes 2308

commit v3 on v2

--- a/solution.py
+++ b/solution.py
@@ -56,9 +56,9 @@
     out_ref, app_ref, xrecv, gain_row,
     wq, wkv, wo, kb, vb, xn, sqcol, sqs, ohs, ohr, live, perm, permt,
     qps, qpr, kps, kpr, qp, qsend, qrecv, kvs, appr, nkv, osend, orecv,
-    lsend, lrecv, asend, arecv, acc, psend, precv, zsend, zrecv,
+    asend, arecv, acc, psend, precv, zsend, zrecv,
     load_sem, sq_s, sq_r, oh_s, oh_r, qp_s, qp_r, kp_s, kp_r, q_s, q_r,
-    app_s, app_r, nk_s, nk_r, o_s, o_r, l_s, l_r, a_s, a_r,
+    app_s, app_r, nk_s, nk_r, o_s, o_r, a_s, a_r,
     p_s, p_r, z_s, z_r, x_s, x_r,
 ):
     gx = lax.axis_index("gx")
@@ -329,18 +329,21 @@
         held = mass > 0.0
         mass = jnp.where(held, mass, 1.0)
         lse = jnp.where(held, top + jnp.log(mass), neg_fill)
-        back = dot(permt[...], (value / mass).astype(bf16))
+        high = lse.astype(bf16).astype(f32)
+        middle = (lse - high).astype(bf16).astype(f32)
+        low = lse - high - middle
+        place = iota((256, 128), 1) - 3 * ((iota((256, 128), 0) >> 3) & 3)
+        parts = jnp.where(
+            place == 0, high, jnp.where(place == 1, middle, jnp.where(place == 2, low, 0.0))
+        )
+        sent = jnp.concatenate([(value / mass).astype(bf16), parts.astype(bf16)], axis=1)
+        back = dot(permt[...], sent)
+        extra = back[0:64, 128:] + back[64:128, 128:] + back[128:192, 128:] + back[192:, 128:]
+        osend[block, :, STEPS * HEAD :] = extra.reshape(8, SLOTS, HEAD).astype(bf16)
         for t in range(STEPS):
             osend[block, :, HEAD * t : HEAD * t + HEAD] = (
-                back[64 * t : 64 * t + 64].reshape(8, SLOTS, HEAD).astype(bf16)
+                back[64 * t : 64 * t + 64, 0:128].reshape(8, SLOTS, HEAD).astype(bf16)
             )
-        packed = jnp.zeros((8, 128), f32)
-        for i in range(32):
-            column = jnp.broadcast_to(lse[8 * i : 8 * i + 8], (8, 128))
-            packed = jnp.where(lane8 == i, column, packed)
-        for i in range(8):
-            lsend[8 * j + i] = packed[i : i + 1]
-
         def one(i, c):
             peer = j * 8 + i
 
@@ -348,7 +351,6 @@
             def _():
                 dev = (gx, peer // 4, lax.rem(peer, 4))
                 remote(osend.at[peer], orecv.at[me], o_s, o_r, dev).start()
-                remote(lsend.at[peer], lrecv.at[me], l_s, l_r, dev).start()
 
             return c
 
@@ -356,7 +358,6 @@
 
     lax.fori_loop(0, ZN, attend, 0)
     orecv[me] = osend[me]
-    lrecv[me] = lsend[me]
 
     def wait_new(i, carry):
         sgy = gy // 2 + 8 * (i // 4)
@@ -389,20 +390,11 @@
     )
     mine = held_by > 0.5
 
-    drain(lrecv.at[pl.ds(0, PEERS - 1)], l_r)
-    spread = jnp.broadcast_to(lrecv[...], (PEERS, SLOTS, 128)).reshape(512, 128)
-    slot_of = iota((512, 128), 0) & 7
-    lane512 = iota((512, 128), 1)
-    table = jnp.zeros((512, 128), f32)
+    drain(orecv.at[pl.ds(0, PEERS - 1)], o_r)
+    table = jnp.transpose(orecv[:, :, STEPS * HEAD :].astype(f32).reshape(512, 128))
     for t in range(STEPS):
-        column = jnp.sum(
-            jnp.where(lane512 == slot_of * 4 + t, spread, 0.0), axis=1, keepdims=True
-        )
-        table = jnp.where(lane512 == t, column, table)
-    table = jnp.transpose(table)
-    drain(orecv.at[pl.ds(0, PEERS - 1)], o_r)
-    for t in range(STEPS):
-        lse = jnp.where(mine, table[t : t + 1, :], neg_fill)
+        lse = table[3 * t : 3 * t + 1] + table[3 * t + 1 : 3 * t + 2] + table[3 * t + 2 : 3 * t + 3]
+        lse = jnp.where(mine, lse, neg_fill)
         top = jnp.max(lse, axis=1, keepdims=True)
         for v in range(t + 1):
             top = jnp.maximum(top, fresh[t, v])
@@ -515,7 +507,6 @@
     drain(ohr.at[pl.ds(0, PEERS - 1)], oh_s)
     drain(qsend.at[pl.ds(0, PEERS - 1)], q_s)
     drain(osend.at[pl.ds(0, PEERS - 1)], o_s)
-    drain(lsend.at[pl.ds(0, PEERS - 1)], l_s)
 
     def sent16(i, carry):
         @pl.when(i != 4 * gx + sa)
@@ -593,14 +584,13 @@
             V((128, 512), bf16),
             V((PEERS, SLOTS, 512), bf16), V((PEERS, SLOTS, 512), bf16),
             V((MEMBERS, HEAD), bf16), V((4, MEMBERS, HEAD), bf16), V((8, MEMBERS, HEAD), bf16),
-            V((PEERS, SLOTS, 512), bf16), V((PEERS, SLOTS, 512), bf16),
-            V((PEERS, 1, 128), f32), V((PEERS, 1, 128), f32),
+            V((PEERS, SLOTS, 640), bf16), V((PEERS, SLOTS, 640), bf16),
             V((STEPS, MEMBERS, HEAD), bf16), V((GROUPS, MEMBERS, 512), bf16),
             V((ZN, ROWS, HEAD), f32), V((ZN, ROWS, HEAD), f32), V((ZN, ROWS, HEAD), f32),
             V((ZN, ROWS, HEAD), bf16), V((ZN, ROWS, HEAD), bf16),
             dma((5,)), dma((3,)), dma((4,)), dma, dma, dma((16,)), dma((16,)), dma((4,)),
             dma((4,)), dma, dma((8,)), dma((3,)), dma((4,)), dma((8,)), dma((8,)),
-            dma, dma, dma, dma, dma((16,)), dma((16,)), dma((8,)), dma((8,)), dma((8,)),
+            dma, dma, dma((16,)), dma((16,)), dma((8,)), dma((8,)), dma((8,)),
             dma((8,)), dma((3,)), dma((4,)),
         ],
         compiler_params=pltpu.CompilerParams(

time: 91.5 us -> 93.2 us (1.019)
  Pallas kernels: 81.3 us -> 83 us
    pallas_call x1, Pallas kernels: 81.3 us -> 83 us  [local(): pl.pallas_call(kernel, out_shape=(jax.ShapeDtypeStruct((STEPS * ROWS, HEA...]
where the time goes in v3:
time: 93.2 us; the launch traced here: 93 us
  Pallas kernels  83 us (89%)
  local copies, waits for them, and re-layouts  8.16 us (9%)
  other arithmetic  1.13 us (1%)
    pallas_call x1, Pallas kernels, local(): pl.pallas_call(kernel, out_shape=(jax.ShapeDtypeStruct((STEPS * ROWS, HEA...  83 us
    unnamed x7, local copies, waits for them, and re-layouts  6.43 us

profile of v3, /device:TPU:1, one launch (start us, length us, event | category | flops | bytes accessed | tf_op | source)
XLA Modules:
  0.0 93.0 jit_solution(8882840683595645549)
XLA Ops:
  0.6 0.0 copy-start
  0.6 1.9 %copy-done = bf16[192,4,2048]{2,1,0:T(4,128)(2,1)S(1)} copy-done((bf16[192,4,2048]{2,1,0:T(4,128)(2,1)S(1)}, bf16[192,4,2048]{2,1,0:T(4,128)(2,1)}, u32[]{:S(2)}) %copy-start) | copy-done | bytes 3145752
  2.5 0.0 copy-start.1
  2.5 1.7 %constant_dynamic-slice_fusion = bf16[192,1,2048]{2,1,0:T(2,128)(2,1)S(1)} fusion(bf16[192,4,2048]{2,1,0:T(4,128)(2,1)S(1)} %copy-done, s32[]{:T(128)S(6)} %select_n.43), kind=kLoop, calls=%fused_computation.24 | loop fusion | bytes 1572868 | tf_op jit(solution)/shard_map/jit(dynamic_index_in_dim)/dynamic_slice | solution.py:552
  4.2 1.3 %copy.15 = bf16[192,1,2048]{2,0,1:T(8,128)(2,1)} copy(bf16[192,1,2048]{2,1,0:T(2,128)(2,1)S(1)} %constant_dynamic-slice_fusion) | data formatting | bytes 1572864
  5.5 0.0 copy-done.1
  5.6 0.1 dynamic_slice.8
  5.6 1.1 %negate_select_fusion = (f32[48,512]{1,0:T(8,128)}, f32[48,512]{1,0:T(8,128)}) fusion(f32[512]{0:T(512)S(1)} %fusion.7, s32[512]{0:T(512)S(1)} %add_select_fusion.1, s32[48]{0:T(128)S(1)} %dynamic_slice.8, pred[512]{0:T(512)(128)(4,1)S(1)} %fusion.8), kind=kLoop, calls=%fused_computation.1 | loop fusion | flops 122880 | bytes 201408 | tf_op jit(solution)/shard_map/jit(_where)/select_n | solution.py:560
  6.8 83.0 %paged_attention_layer.1 = (f32[768,128]{1,0:T(8,128)}, bf16[192,128]{1,0:T(8,128)(2,1)}) custom-call(bf16[192,2048]{1,0:T(8,128)(2,1)} %bitcast.6, bf16[16,128]{1,0:T(8,128)(2,1)} %bitcast.9, f32[48,512]{1,0:T(8,128)} %get-tuple-element.7.cos_ref, f32[48,512]{1,0:T(8,128)} %get-tuple-element.6.sin_ref, s32[192]{0:T(256)} %len_ref.1, s32[8]{0:T(128)} %own_ref.1, ...), custom_call_target="tpu_custom_call" | custom-call | tf_op jit(solution)/shard_map/paged_attention_layer/pallas_call | solution.py:567
  89.8 1.8 %copy.18 = f32[192,4,128]{2,1,0:T(4,128)} copy(f32[192,4,128]{2,1,0:T(4,128)} %bitcast.7) | data formatting | bytes 786432
  91.5 1.4 %copy.19 = bf16[48,4,128]{2,1,0:T(4,128)(2,1)} copy(bf16[48,4,128]{2,1,0:T(4,128)(2,1)} %bitcast.8) | data formatting | bytes 98304
  (3 shorter events, 0.0 us)
Async XLA Ops:
  0.6 1.9 %copy-start = (bf16[192,4,2048]{2,1,0:T(4,128)(2,1)S(1)}, bf16[192,4,2048]{2,1,0:T(4,128)(2,1)}, u32[]{:S(2)}) copy-start(bf16[192,4,2048]{2,1,0:T(4,128)(2,1)} %param.10) | copy-start | bytes 9437188
  2.5 3.0 %copy-start.1 = (s32[192]{0:T(256)S(1)}, s32[192]{0:T(256)}, u32[]{:S(2)}) copy-start(s32[192]{0:T(256)} %len_ref.1) | copy-start | bytes 2308
